TPU v7x, 32 devices: a whole 2x2x4 slice. The times are simulated.
32 devices in a mesh: groups: 2 (over y), tok: 16 (over z, x, core).
Axes of the slice: x: 2, y: 2, z: 4, core: 2. Of those that a mesh axis runs over, the one named last changes fastest.
Arguments:
- queries: bfloat16 [1024, 2048], P(('groups', 'tok')), parts along dimension 0, may hold values from -6 to 6
- new_kv: bfloat16 [3072, 4096], P(('groups', 'tok')), parts along dimension 0, may hold values from -6 to 6
- prev_kv: bfloat16 [2, 3072, 4096], P(None, ('groups', 'tok')), parts along dimension 1, may hold values from -6 to 6
- base_step: int32 [32], P(('groups', 'tok')), parts along dimension 0, may hold values from 0 to 1
- live_counts: int32 [32], P('groups'), parts along dimension 0, may hold values from 1 to 96
- sketch: float32 [4096, 32], replicated, may hold values from -0.09375 to 0.09375
- cache: bfloat16 [64, 1536, 128], P(('groups', 'tok')), parts along dimension 0, may hold values from -6 to 6, as said below
- w_out: bfloat16 [2048, 1536], replicated, may hold values from -0.125 to 0.125
Outputs:
- projected: bfloat16 [1024, 1536], P(('groups', 'tok')), parts along dimension 0
There are 2 independent parts, one for each index of `groups`. A program takes and returns all parts, laid end to end along the dimension named above; an argument that names none is the same for every part. Nothing has to cross between parts.
Inputs may be any that keep to these rules, and one draw needn't show every extreme that they name: cache slots i and j hold the same values when i // 2 == j // 2 and i % 2 == j % 2.
All inputs are finite; a program needn't handle non-finite values.
Results may differ from a plain program's by a relative error of at most 0.019.
Values may be sent and summed in bfloat16 or wider, within the bound.
No kernel may reach another device: no remote copies, remote signals or barrier semaphores. Data moves between devices by JAX's collectives and lax.ppermute only.
A program may use at most 128 MiB of HBM per device.

v0:
```python
import math
import jax
import jax.numpy as jnp
from jax import lax
from jax.sharding import PartitionSpec as P

HD = 64
SWEEPS = 2
highest = lax.Precision.HIGHEST


def orthonormal(block_cols):
    gram_matrix = jnp.dot(block_cols.T, block_cols, precision=highest)
    lower_factor = jnp.linalg.cholesky(gram_matrix)
    return jax.scipy.linalg.solve_triangular(lower_factor, block_cols.T, lower=True).T


def compress(delta_block, sketch):
    basis_cols = orthonormal(jnp.dot(delta_block, sketch, precision=highest))
    for sweep_index in range(SWEEPS):
        inner = jnp.dot(delta_block.T, basis_cols, precision=highest)
        basis_cols = orthonormal(jnp.dot(delta_block, inner, precision=highest))
    right_factor = jnp.dot(basis_cols.T, delta_block, precision=highest)
    return (basis_cols.astype(jnp.bfloat16), right_factor.astype(jnp.bfloat16))


def spread_heads(matrix, head_groups, groups_q, width):
    lead = matrix.shape[0]
    per_group = matrix.reshape(lead, head_groups, width).transpose(1, 0, 2)
    copies = jnp.broadcast_to(per_group[:, None], (head_groups, groups_q, lead, width))
    return copies.reshape(head_groups * groups_q, lead, width)


def attend_head(pieces, live_keys):
    q_head, keys_values = pieces
    key_part = keys_values[:, :HD]
    value_part = keys_values[:, HD:]
    query_count = q_head.shape[0]
    block_rows = math.gcd(query_count, 512)

    def one_block(query_block):
        scores = jnp.dot(query_block, key_part.T, preferred_element_type=jnp.float32) * HD ** (-0.5)
        scores = jnp.where(live_keys[None, :], scores, -1e30)
        row_max = jnp.max(scores, axis=-1, keepdims=True)
        exponent = jnp.exp(scores - row_max)
        weights = (exponent / jnp.sum(exponent, axis=-1, keepdims=True)).astype(jnp.bfloat16)
        return jnp.dot(weights, value_part, preferred_element_type=jnp.float32).astype(jnp.bfloat16)

    return lax.map(one_block, q_head.reshape(query_count // block_rows, block_rows, HD)).reshape(
        query_count, HD
    )


def per_device(queries, new_kv, prev_kv, base_step, live_counts, sketch, cache, w_out):
    shards = lax.axis_size("tok")
    tok_rows = new_kv.shape[0]
    query_rows = queries.shape[0]
    head_count = queries.shape[1] // HD
    groups_q = max(1, shards // head_count)
    per_dev = head_count * groups_q // shards
    head_groups = head_count // per_dev
    part_rows = query_rows // groups_q
    width = per_dev * 2 * HD
    key_count = shards * tok_rows
    query_count = shards * part_rows
    prior = prev_kv[0].astype(jnp.float32)
    prior = jnp.where(base_step[0] == 1, prev_kv[1].astype(jnp.float32), prior)
    delta = new_kv.astype(jnp.float32) - prior
    left_factor, right_factor = compress(delta, sketch)
    rank_cols = left_factor.shape[1]
    q_blocks = queries.reshape(groups_q, part_rows, head_groups, per_dev * HD)
    q_blocks = q_blocks.transpose(2, 0, 1, 3).reshape(shards, part_rows, per_dev * HD)
    w_blocks = spread_heads(right_factor, head_groups, groups_q, width)
    q_here = lax.all_to_all(q_blocks, "tok", split_axis=0, concat_axis=0, tiled=True)
    u_here = lax.all_gather(left_factor, "tok", axis=0, tiled=True).reshape(
        shards, tok_rows, rank_cols
    )
    w_here = lax.all_to_all(w_blocks, "tok", split_axis=0, concat_axis=0, tiled=True)
    lowrank = jnp.einsum("str,src->stc", u_here, w_here, preferred_element_type=jnp.float32).astype(
        jnp.bfloat16
    )
    lowrank = lowrank.reshape(key_count, per_dev, 2 * HD).transpose(1, 0, 2)
    keys_values = (cache.astype(jnp.float32) + lowrank.astype(jnp.float32)).astype(jnp.bfloat16)
    live_keys = (jnp.arange(tok_rows, dtype=jnp.int32)[None, :] < live_counts[:, None]).reshape(
        key_count
    )
    q_heads = q_here.reshape(query_count, per_dev, HD).transpose(1, 0, 2)
    attended = lax.map(lambda pieces: attend_head(pieces, live_keys), (q_heads, keys_values))
    attended = attended.transpose(1, 0, 2).reshape(shards, part_rows, per_dev * HD)
    returned = lax.all_to_all(attended, "tok", split_axis=0, concat_axis=0, tiled=True)
    returned = returned.reshape(head_groups, groups_q, part_rows, per_dev * HD)
    row_block = returned.transpose(1, 2, 0, 3).reshape(query_rows, head_count * HD)
    return jnp.dot(row_block, w_out, preferred_element_type=jnp.float32).astype(jnp.bfloat16)


def solution(mesh):
    return jax.shard_map(
        per_device,
        mesh=mesh,
        in_specs=(
            P(("groups", "tok"), None),
            P(("groups", "tok"), None),
            P(None, ("groups", "tok"), None),
            P(("groups", "tok")),
            P("groups"),
            P(),
            P(("groups", "tok"), None, None),
            P(),
        ),
        out_specs=P(("groups", "tok"), None),
        check_vma=False,
    )
```

profile of v0, /device:TPU:0, one launch (start us, length us, event | category | flops | bytes accessed | tf_op | source)
XLA Modules:
  0.0 94.7 jit_solution(8483638808945009714)
XLA Ops:
  0.0 1.0 %copy.33 = bf16[4,8,16,128]{3,2,1,0:T(8,128)(2,1)S(1)} copy(bf16[4,8,16,128]{3,1,2,0:T(8,128)(2,1)} %bitcast.116) | data formatting | bytes 262144
  1.0 0.7 copy.43
  1.7 7.4 %all-to-all-start = ((bf16[16,32,128]{2,1,0:T(8,128)(2,1)}), bf16[16,32,128]{2,1,0:T(8,128)(2,1)S(1)}, u32[]{:S(2)}, u32[]{:S(2)}) async-start(bf16[16,32,128]{2,1,0:T(8,128)(2,1)} %bitcast.103), calls=%async_computation | async-start | bytes 262144 | tf_op jit(solution)/shard_map/all_to_all | solution.py:74
  9.7 1.9 %bitcast_subtract_fusion = f32[96,4096]{1,0:T(8,128)S(1)} fusion(bf16[96,4096]{1,0:T(8,128)(2,1)} %param.14, bf16[2,96,4096]{2,1,0:T(8,128)(2,1)} %param.15, pred[]{:T(512)} %bitcast.3), kind=kLoop, calls=%fused_computation.21 | loop fusion | flops 1966080 | bytes 3932161 | tf_op jit(solution)/shard_map/sub | solution.py:68
  11.6 1.3 %fusion.37 = f32[96,32]{0,1:T(8,128)S(1)} fusion(f32[96,4096]{1,0:T(8,128)S(1)} %bitcast_subtract_fusion, f32[4096,32]{0,1:T(8,128)S(1)} %copy-done), kind=kOutput, calls=%fused_computation.61 | convolution fusion | flops 150994944 | bytes 2109440 | tf_op jit(solution)/shard_map/dot_general | solution.py:19
  13.0 0.1 fusion.38
  13.2 2.9 %cholesky.59 = f32[32,32]{1,0:T(8,128)S(1)} custom-call(f32[32,32]{1,0:T(8,128)S(1)} %fusion.31), custom_call_target="Cholesky" | custom-call | tf_op jit(solution)/shard_map/jit(cholesky)/cholesky | solution.py:14
  16.2 0.6 compare_reduce_fusion.2
  16.8 0.7 fusion.17
  17.5 2.4 %custom-call.7 = f32[1,32,32]{1,2,0:T(8,128)S(1)} custom-call(f32[1,32,32]{2,1,0:T(8,128)S(1)} %fusion.17), custom_call_target="InvertDiagBlocksLowerTriangular" | custom-call | tf_op jit(solution)/shard_map/jit(_solve_triangular)/triangular_solve | solution.py:15
  19.9 0.2 fusion.28
  20.1 1.0 %fusion.39 = f32[4096,32]{0,1:T(8,128)S(1)} fusion(f32[96,4096]{1,0:T(8,128)S(1)} %bitcast_subtract_fusion, f32[32,96]{1,0:T(8,128)S(1)} %fusion.28), kind=kOutput, calls=%fused_computation.63 | convolution fusion | flops 150994944 | bytes 2109440 | tf_op jit(solution)/shard_map/dot_general | solution.py:21
  21.2 1.3 %fusion.40 = f32[96,32]{0,1:T(8,128)S(1)} fusion(f32[96,4096]{1,0:T(8,128)S(1)} %bitcast_subtract_fusion, f32[4096,32]{0,1:T(8,128)S(1)} %fusion.39), kind=kOutput, calls=%fused_computation.64 | convolution fusion | flops 150994944 | bytes 2109440 | tf_op jit(solution)/shard_map/dot_general | solution.py:22
  22.5 0.1 fusion.41
  22.7 2.9 %cholesky.70 = f32[32,32]{1,0:T(8,128)S(1)} custom-call(f32[32,32]{1,0:T(8,128)S(1)} %fusion.27), custom_call_target="Cholesky" | custom-call | tf_op jit(solution)/shard_map/jit(cholesky)/cholesky | solution.py:14
  25.7 0.6 compare_reduce_fusion.1
  26.3 0.7 fusion.18
  27.0 2.4 %custom-call.8 = f32[1,32,32]{1,2,0:T(8,128)S(1)} custom-call(f32[1,32,32]{2,1,0:T(8,128)S(1)} %fusion.18), custom_call_target="InvertDiagBlocksLowerTriangular" | custom-call | tf_op jit(solution)/shard_map/jit(_solve_triangular)/triangular_solve | solution.py:15
  29.4 0.2 fusion.24
  29.7 1.0 %fusion.42 = f32[4096,32]{0,1:T(8,128)S(1)} fusion(f32[96,4096]{1,0:T(8,128)S(1)} %bitcast_subtract_fusion, f32[32,96]{1,0:T(8,128)S(1)} %fusion.24), kind=kOutput, calls=%fused_computation.66 | convolution fusion | flops 150994944 | bytes 2109440 | tf_op jit(solution)/shard_map/dot_general | solution.py:21
  30.7 1.3 %fusion.43 = f32[96,32]{0,1:T(8,128)S(1)} fusion(f32[96,4096]{1,0:T(8,128)S(1)} %bitcast_subtract_fusion, f32[4096,32]{0,1:T(8,128)S(1)} %fusion.42), kind=kOutput, calls=%fused_computation.67 | convolution fusion | flops 150994944 | bytes 2109440 | tf_op jit(solution)/shard_map/dot_general | solution.py:22
  32.0 0.1 fusion.44
  32.3 2.9 %cholesky.81 = f32[32,32]{1,0:T(8,128)S(1)} custom-call(f32[32,32]{1,0:T(8,128)S(1)} %fusion.23), custom_call_target="Cholesky" | custom-call | tf_op jit(solution)/shard_map/jit(cholesky)/cholesky | solution.py:14
  35.2 0.6 compare_reduce_fusion
  35.9 0.7 fusion.19
  36.5 2.4 %custom-call.9 = f32[1,32,32]{1,2,0:T(8,128)S(1)} custom-call(f32[1,32,32]{2,1,0:T(8,128)S(1)} %fusion.19), custom_call_target="InvertDiagBlocksLowerTriangular" | custom-call | tf_op jit(solution)/shard_map/jit(_solve_triangular)/triangular_solve | solution.py:15
  39.0 0.2 fusion.20
  39.2 0.9 convolution_convert_fusion
  40.1 0.7 copy.42
  40.8 6.0 %all-to-all-start.1 = ((bf16[16,32,256]{2,1,0:T(8,128)(2,1)}), bf16[16,32,256]{2,1,0:T(8,128)(2,1)S(1)}, u32[]{:S(2)}, u32[]{:S(2)}) async-start(bf16[16,32,256]{2,1,0:T(8,128)(2,1)} %bitcast.102), calls=%async_computation.1 | async-start | bytes 524288 | tf_op jit(solution)/shard_map/all_to_all | solution.py:78
  46.8 22.3 %all-gather = bf16[16,96,32]{1,2,0:T(8,128)(2,1)S(1)} all-gather(bf16[1,96,32]{1,2,0:T(8,128)(2,1)S(1)} %convert_bitcast_fusion), channel_id=1, replica_groups=mesh['groups'=2,'tok'=16] {'tok'}, dimensions={0}, use_global_device_ids=true | all-gather | bytes 104448 | tf_op jit(solution)/shard_map/all_gather | solution.py:75
  69.2 0.1 reshape.49
  69.4 1.6 %fusion.14 = f32[16,96,256]{2,1,0:T(8,128)} fusion(bf16[16,96,32]{1,2,0:T(8,128)(2,1)S(1)} %all-gather, bf16[16,32,256]{2,1,0:T(8,128)(2,1)S(1)} %all-to-all-done.1), kind=kOutput, calls=%fused_computation.23 | convolution fusion | flops 25952256 | bytes 1933312 | tf_op jit(solution)/shard_map/str,src->stc/dot_general | solution.py:79
  71.0 2.1 %reshape.55 = f32[1536,2,128]{2,1,0:T(2,128)S(1)} reshape(f32[16,96,256]{2,1,0:T(8,128)} %fusion.14) | data formatting | bytes 3145728 | tf_op jit(solution)/shard_map/convert_element_type | solution.py:83
  73.0 1.3 %fusion.13 = bf16[2,1536,128]{2,1,0:T(8,128)(2,1)S(1)} fusion(f32[1536,2,128]{2,1,0:T(2,128)S(1)} %reshape.55, bf16[2,1536,128]{2,1,0:T(8,128)(2,1)} %param.19), kind=kLoop, calls=%fused_computation.20 | loop fusion | flops 1179648 | bytes 3145728 | tf_op jit(solution)/shard_map/convert_element_type | solution.py:83
  74.3 4.9 %while.11 = (s32[]{:T(128)}, bf16[2,512,64]{1,2,0:T(8,128)(2,1)S(1)}, bf16[2,512,64]{2,1,0:T(8,128)(2,1)S(1)}, bf16[2,1536,128]{2,1,0:T(8,128)(2,1)S(1)}, s32[16]{0:T(128)S(1)}, /*index=5*/s32[]{:T(128)}) while((s32[]{:T(128)}, bf16[2,512,64]{1,2,0:T(8,128)(2,1)S(1)}, bf16[2,512,64]{2,1,0:T(8,128)(2,1)S(1)}, ...), condition=%wide.region_5.8_spmd.clone, body=%wide.region_2.7_spmd.clone.sunk | while | flops 207651328 | bytes 11223697 | solution.py:88
  74.5 0.1 broadcast_in_dim.43
  74.5 0.7 fusion.71
  75.2 0.6 fusion.72
  75.8 1.0 %fusion.73 = bf16[2,512,64]{1,2,0:T(8,128)(2,1)S(1)} fusion(bf16[2,512,64]{1,2,0:T(8,128)(2,1)S(1)} %get-tuple-element.130, s32[]{:T(128)} %get-tuple-element.129, f32[512,1536]{1,0:T(8,128)S(1)} %get-tuple-element.121, f32[512]{0:T(512)S(1)} %fusion.72, f32[512]{0:T(512)S(1)} %get-tuple-element.122, ...), kind=kOutput, calls=%fused_computation.9.clone.1 | convolution fusion | flops 103055360 | bytes 3608580 | tf_op jit(solution)/shard_map/while/body/eval_jaxpr/while/body/eval_jaxpr/dot_general | solution.py:47
  76.9 0.1 broadcast_in_dim.43
  77.0 0.7 fusion.71
  77.7 0.6 fusion.72
  78.3 1.0 %fusion.73 = bf16[2,512,64]{1,2,0:T(8,128)(2,1)S(1)} fusion(bf16[2,512,64]{1,2,0:T(8,128)(2,1)S(1)} %get-tuple-element.130, s32[]{:T(128)} %get-tuple-element.129, f32[512,1536]{1,0:T(8,128)S(1)} %get-tuple-element.121, f32[512]{0:T(512)S(1)} %fusion.72, f32[512]{0:T(512)S(1)} %get-tuple-element.122, ...), kind=kOutput, calls=%fused_computation.9.clone.1 | convolution fusion | flops 103055360 | bytes 3608580 | tf_op jit(solution)/shard_map/while/body/eval_jaxpr/while/body/eval_jaxpr/dot_general | solution.py:47
  79.3 0.2 copy.30
  79.4 0.1 reshape.52
  79.6 10.5 %all_to_all.15 = bf16[16,32,128]{2,1,0:T(8,128)(2,1)S(1)} all-to-all(bf16[16,32,128]{2,1,0:T(8,128)(2,1)S(1)} %reshape.52), channel_id=1, replica_groups=mesh['groups'=2,'tok'=16] {'tok'}, dimensions={0} | all-to-all | bytes 262144 | tf_op jit(solution)/shard_map/all_to_all | solution.py:90
  90.1 4.6 %convolution_convert_fusion.1 = bf16[32,1536]{1,0:T(8,128)(2,1)} fusion(bf16[2048,1536]{1,0:T(8,128)(2,1)} %param.20, bf16[4,8,16,128]{3,2,1,0:T(8,128)(2,1)S(1)} %bitcast.112), kind=kOutput, calls=%fused_computation.18 | convolution fusion | flops 201375744 | bytes 6520832 | tf_op jit(solution)/shard_map/dot_general | solution.py:93
  (23 shorter events, 0.7 us)
Async XLA Ops:
  0.0 11.6 %copy-start = (f32[4096,32]{0,1:T(8,128)S(1)}, f32[4096,32]{0,1:T(8,128)}, u32[]{:S(2)}) copy-start(f32[4096,32]{0,1:T(8,128)} %param.18) | copy-start | bytes 1572868
  1.7 39.1 %all-to-all-start = ((bf16[16,32,128]{2,1,0:T(8,128)(2,1)}), bf16[16,32,128]{2,1,0:T(8,128)(2,1)S(1)}, u32[]{:S(2)}, u32[]{:S(2)}) async-start(bf16[16,32,128]{2,1,0:T(8,128)(2,1)} %bitcast.103), calls=%async_computation | async-start | bytes 262144 | tf_op jit(solution)/shard_map/all_to_all | solution.py:74
  40.8 28.6 %all-to-all-start.1 = ((bf16[16,32,256]{2,1,0:T(8,128)(2,1)}), bf16[16,32,256]{2,1,0:T(8,128)(2,1)S(1)}, u32[]{:S(2)}, u32[]{:S(2)}) async-start(bf16[16,32,256]{2,1,0:T(8,128)(2,1)} %bitcast.102), calls=%async_computation.1 | async-start | bytes 524288 | tf_op jit(solution)/shard_map/all_to_all | solution.py:78
  73.0 1.3 %copy-start.1 = (s32[16]{0:T(128)S(1)}, s32[16]{0:T(128)}, u32[]{:S(2)}) copy-start(s32[16]{0:T(128)} %param.17) | copy-start | bytes 196
where the time goes:
time: 95.2 us; the launch traced here: 94.7 us
  blocking collectives  32.8 us (34%)
  other arithmetic  24.6 us (26%)
  matrix products  17.5 us (18%)
  starting transfers between devices  13.4 us (14%)
  local copies, waits for them, and re-layouts  5.45 us (6%)
    all_gather x1, blocking collectives, per_device(): lax.all_gather(left_factor, 'tok', axis=0, tiled=True)  22.3 us
    another operation x9, other arithmetic, orthonormal(): lower_factor = jnp.linalg.cholesky(gram_matrix)  10.8 us
    all_to_all x1, blocking collectives, per_device(): lax.all_to_all(attended, 'tok', split_axis=0, concat_axis=0, tiled=True)  10.5 us
    another operation x6, other arithmetic, orthonormal(): jax.scipy.linalg.solve_triangular(lower_factor, block_cols.T, lower=True)  9.26 us
    all_to_all x1, starting transfers between devices, per_device(): lax.all_to_all(q_blocks, 'tok', split_axis=0, concat_axis=0, tiled=True)  7.39 us
    all_to_all x1, starting transfers between devices, per_device(): lax.all_to_all(w_blocks, 'tok', split_axis=0, concat_axis=0, tiled=True)  6.01 us
    dot_general x1, matrix products, per_device(): jnp.dot(row_block, w_out, preferred_element_type=jnp.float32)  4.56 us
    dot_general x2, matrix products, compress(): basis_cols = orthonormal(jnp.dot(delta_block, inner, precision=highest))  2.69 us
  transfers between devices with their start and end apart: 2, of which 0 were waited for; matrix products, arithmetic and copies ran while one was open for 33% of the time, Pallas kernels for 0%

commit v1 on v0

--- a/solution.py
+++ b/solution.py
@@ -7,6 +7,11 @@
 HD = 64
 SWEEPS = 2
 highest = lax.Precision.HIGHEST
+
+
+def swapped_in(x, axis, dim):
+    stack = jnp.stack([x] * lax.axis_size(axis))
+    return jnp.concatenate(lax.all_to_all(stack, axis, 0, 0), axis=dim)
 
 
 def orthonormal(block_cols):
@@ -72,9 +77,7 @@
     q_blocks = q_blocks.transpose(2, 0, 1, 3).reshape(shards, part_rows, per_dev * HD)
     w_blocks = spread_heads(right_factor, head_groups, groups_q, width)
     q_here = lax.all_to_all(q_blocks, "tok", split_axis=0, concat_axis=0, tiled=True)
-    u_here = lax.all_gather(left_factor, "tok", axis=0, tiled=True).reshape(
-        shards, tok_rows, rank_cols
-    )
+    u_here = swapped_in(left_factor, "tok", 0).reshape(shards, tok_rows, rank_cols)
     w_here = lax.all_to_all(w_blocks, "tok", split_axis=0, concat_axis=0, tiled=True)
     lowrank = jnp.einsum("str,src->stc", u_here, w_here, preferred_element_type=jnp.float32).astype(
         jnp.bfloat16

time: 95.2 us -> 97.1 us (1.020)
  waiting for transfers between devices: 0.01 us -> 23.1 us
  blocking collectives: 32.8 us -> 10.7 us
  starting transfers between devices: 13.4 us -> 14.6 us
    all_gather x1 -> x0, blocking collectives: 22.3 us -> none  [per_device(): lax.all_gather(left_factor, 'tok', axis=0, tiled=True)]
    all_to_all x1, waiting for transfers between devices: 0.01 us -> 9.6 us  [per_device(): lax.all_to_all(w_blocks, 'tok', split_axis=0, concat_axis=0, tiled=True)]
    all_to_all x0 -> x1, starting transfers between devices: none -> 7.39 us  [swapped_in(): return jnp.concatenate(lax.all_to_all(stack, axis, 0, 0), axis=dim)]
    all_to_all x0 -> x1, waiting for transfers between devices: none -> 7.17 us  [swapped_in(): return jnp.concatenate(lax.all_to_all(stack, axis, 0, 0), axis=dim)]
    all_to_all x1, waiting for transfers between devices: 0.01 us -> 6.28 us  [per_device(): lax.all_to_all(q_blocks, 'tok', split_axis=0, concat_axis=0, tiled=True)]
    all_to_all x1, starting transfers between devices: 7.39 us -> 3.51 us  [per_device(): lax.all_to_all(q_blocks, 'tok', split_axis=0, concat_axis=0, tiled=True)]
    all_to_all x1, starting transfers between devices: 6.01 us -> 3.71 us  [per_device(): lax.all_to_all(w_blocks, 'tok', split_axis=0, concat_axis=0, tiled=True)]
  transfers between devices with their start and end apart: 2 -> 3, of which waited for: 0 -> 3; matrix products, arithmetic and copies ran while one was open for 33% -> 3% of each run, Pallas kernels for 0% -> 0%
where the time goes in v1:
time: 97.1 us; the launch traced here: 96.6 us
  other arithmetic  24.6 us (25%)
  waiting for transfers between devices  23.1 us (24%)
  matrix products  17.5 us (18%)
  starting transfers between devices  14.6 us (15%)
  blocking collectives  10.7 us (11%)
  local copies, waits for them, and re-layouts  5.15 us (5%)
  between operations  1.01 us (1%)
    another operation x9, other arithmetic, orthonormal(): lower_factor = jnp.linalg.cholesky(gram_matrix)  10.8 us
    all_to_all x1, blocking collectives, per_device(): lax.all_to_all(attended, 'tok', split_axis=0, concat_axis=0, tiled=True)  10.7 us
    all_to_all x1, waiting for transfers between devices, per_device(): lax.all_to_all(w_blocks, 'tok', split_axis=0, concat_axis=0, tiled=True)  9.6 us
    another operation x6, other arithmetic, orthonormal(): jax.scipy.linalg.solve_triangular(lower_factor, block_cols.T, lower=True)  9.26 us
    all_to_all x1, starting transfers between devices, swapped_in(): return jnp.concatenate(lax.all_to_all(stack, axis, 0, 0), axis=dim)  7.39 us
    all_to_all x1, waiting for transfers between devices, swapped_in(): return jnp.concatenate(lax.all_to_all(stack, axis, 0, 0), axis=dim)  7.17 us
    all_to_all x1, waiting for transfers between devices, per_device(): lax.all_to_all(q_blocks, 'tok', split_axis=0, concat_axis=0, tiled=True)  6.28 us
    dot_general x1, matrix products, per_device(): jnp.dot(row_block, w_out, preferred_element_type=jnp.float32)  4.56 us
  transfers between devices with their start and end apart: 3, of which 3 were waited for; matrix products, arithmetic and copies ran while one was open for 3% of the time, Pallas kernels for 0%

profile of v1, /device:TPU:0, one launch (start us, length us, event | category | flops | bytes accessed | tf_op | source)
XLA Modules:
  0.0 96.6 jit_solution(9562710304180005357)
XLA Ops:
  0.7 1.9 %bitcast_subtract_fusion = f32[96,4096]{1,0:T(8,128)S(1)} fusion(bf16[96,4096]{1,0:T(8,128)(2,1)} %param.14, bf16[2,96,4096]{2,1,0:T(8,128)(2,1)} %param.15, pred[]{:T(512)} %bitcast.3), kind=kLoop, calls=%fused_computation.21 | loop fusion | flops 1966080 | bytes 3932161 | tf_op jit(solution)/shard_map/sub | solution.py:73
  2.6 1.3 %fusion.37 = f32[96,32]{0,1:T(8,128)S(1)} fusion(f32[96,4096]{1,0:T(8,128)S(1)} %bitcast_subtract_fusion, f32[4096,32]{0,1:T(8,128)S(1)} %copy-done), kind=kOutput, calls=%fused_computation.61 | convolution fusion | flops 150994944 | bytes 2109440 | tf_op jit(solution)/shard_map/dot_general | solution.py:24
  4.0 0.1 fusion.38
  4.2 2.9 %cholesky.59 = f32[32,32]{1,0:T(8,128)S(1)} custom-call(f32[32,32]{1,0:T(8,128)S(1)} %fusion.31), custom_call_target="Cholesky" | custom-call | tf_op jit(solution)/shard_map/jit(cholesky)/cholesky | solution.py:19
  7.2 0.6 compare_reduce_fusion.2
  7.8 0.7 fusion.17
  8.5 2.4 %custom-call.7 = f32[1,32,32]{1,2,0:T(8,128)S(1)} custom-call(f32[1,32,32]{2,1,0:T(8,128)S(1)} %fusion.17), custom_call_target="InvertDiagBlocksLowerTriangular" | custom-call | tf_op jit(solution)/shard_map/jit(_solve_triangular)/triangular_solve | solution.py:20
  10.9 0.2 fusion.28
  11.1 1.0 %fusion.39 = f32[4096,32]{0,1:T(8,128)S(1)} fusion(f32[96,4096]{1,0:T(8,128)S(1)} %bitcast_subtract_fusion, f32[32,96]{1,0:T(8,128)S(1)} %fusion.28), kind=kOutput, calls=%fused_computation.63 | convolution fusion | flops 150994944 | bytes 2109440 | tf_op jit(solution)/shard_map/dot_general | solution.py:26
  12.1 1.3 %fusion.40 = f32[96,32]{0,1:T(8,128)S(1)} fusion(f32[96,4096]{1,0:T(8,128)S(1)} %bitcast_subtract_fusion, f32[4096,32]{0,1:T(8,128)S(1)} %fusion.39), kind=kOutput, calls=%fused_computation.64 | convolution fusion | flops 150994944 | bytes 2109440 | tf_op jit(solution)/shard_map/dot_general | solution.py:27
  13.5 0.1 fusion.41
  13.7 2.9 %cholesky.70 = f32[32,32]{1,0:T(8,128)S(1)} custom-call(f32[32,32]{1,0:T(8,128)S(1)} %fusion.27), custom_call_target="Cholesky" | custom-call | tf_op jit(solution)/shard_map/jit(cholesky)/cholesky | solution.py:19
  16.7 0.6 compare_reduce_fusion.1
  17.3 0.7 fusion.18
  18.0 2.4 %custom-call.8 = f32[1,32,32]{1,2,0:T(8,128)S(1)} custom-call(f32[1,32,32]{2,1,0:T(8,128)S(1)} %fusion.18), custom_call_target="InvertDiagBlocksLowerTriangular" | custom-call | tf_op jit(solution)/shard_map/jit(_solve_triangular)/triangular_solve | solution.py:20
  20.4 0.2 fusion.24
  20.7 1.0 %fusion.42 = f32[4096,32]{0,1:T(8,128)S(1)} fusion(f32[96,4096]{1,0:T(8,128)S(1)} %bitcast_subtract_fusion, f32[32,96]{1,0:T(8,128)S(1)} %fusion.24), kind=kOutput, calls=%fused_computation.66 | convolution fusion | flops 150994944 | bytes 2109440 | tf_op jit(solution)/shard_map/dot_general | solution.py:26
  21.7 1.3 %fusion.43 = f32[96,32]{0,1:T(8,128)S(1)} fusion(f32[96,4096]{1,0:T(8,128)S(1)} %bitcast_subtract_fusion, f32[4096,32]{0,1:T(8,128)S(1)} %fusion.42), kind=kOutput, calls=%fused_computation.67 | convolution fusion | flops 150994944 | bytes 2109440 | tf_op jit(solution)/shard_map/dot_general | solution.py:27
  23.0 0.1 fusion.44
  23.3 2.9 %cholesky.81 = f32[32,32]{1,0:T(8,128)S(1)} custom-call(f32[32,32]{1,0:T(8,128)S(1)} %fusion.23), custom_call_target="Cholesky" | custom-call | tf_op jit(solution)/shard_map/jit(cholesky)/cholesky | solution.py:19
  26.2 0.6 compare_reduce_fusion
  26.9 0.7 fusion.19
  27.5 2.4 %custom-call.9 = f32[1,32,32]{1,2,0:T(8,128)S(1)} custom-call(f32[1,32,32]{2,1,0:T(8,128)S(1)} %fusion.19), custom_call_target="InvertDiagBlocksLowerTriangular" | custom-call | tf_op jit(solution)/shard_map/jit(_solve_triangular)/triangular_solve | solution.py:20
  30.0 0.2 fusion.20
  30.2 0.7 stack.2
  30.9 7.4 %all-to-all-start.1 = ((bf16[16,96,32]{1,2,0:T(8,128)(2,1)}), bf16[16,96,32]{1,2,0:T(8,128)(2,1)S(1)}, u32[]{:S(2)}, u32[]{:S(2)}) async-start(bf16[16,96,32]{1,2,0:T(8,128)(2,1)} %stack.2), calls=%async_computation.1 | async-start | bytes 262144 | tf_op jit(solution)/shard_map/all_to_all | solution.py:14
  38.3 0.7 copy.43
  39.0 7.2 %all-to-all-done.1 = bf16[16,96,32]{1,2,0:T(8,128)(2,1)S(1)} async-done(((bf16[16,96,32]{1,2,0:T(8,128)(2,1)}), bf16[16,96,32]{1,2,0:T(8,128)(2,1)S(1)}, u32[]{:S(2)}, u32[]{:S(2)}) %all-to-all-start.1) | async-done | bytes 98336 | tf_op jit(solution)/shard_map/all_to_all | solution.py:14
  46.2 3.5 %all-to-all-start = ((bf16[16,32,128]{2,1,0:T(8,128)(2,1)}), bf16[16,32,128]{2,1,0:T(8,128)(2,1)S(1)}, u32[]{:S(2)}, u32[]{:S(2)}) async-start(bf16[16,32,128]{2,1,0:T(8,128)(2,1)} %bitcast.101), calls=%async_computation | async-start | bytes 262144 | tf_op jit(solution)/shard_map/all_to_all | solution.py:79
  49.7 0.9 convolution_convert_fusion
  50.6 0.7 copy.42
  51.3 6.3 %all-to-all-done = bf16[16,32,128]{2,1,0:T(8,128)(2,1)S(1)} async-done(((bf16[16,32,128]{2,1,0:T(8,128)(2,1)}), bf16[16,32,128]{2,1,0:T(8,128)(2,1)S(1)}, u32[]{:S(2)}, u32[]{:S(2)}) %all-to-all-start) | async-done | bytes 131104 | tf_op jit(solution)/shard_map/all_to_all | solution.py:79
  57.6 3.7 %all-to-all-start.2 = ((bf16[16,32,256]{2,1,0:T(8,128)(2,1)}), bf16[16,32,256]{2,1,0:T(8,128)(2,1)S(1)}, u32[]{:S(2)}, u32[]{:S(2)}) async-start(bf16[16,32,256]{2,1,0:T(8,128)(2,1)} %bitcast.100), calls=%async_computation.2 | async-start | bytes 524288 | tf_op jit(solution)/shard_map/all_to_all | solution.py:81
  61.5 9.6 %all-to-all-done.2 = bf16[16,32,256]{2,1,0:T(8,128)(2,1)S(1)} async-done(((bf16[16,32,256]{2,1,0:T(8,128)(2,1)}), bf16[16,32,256]{2,1,0:T(8,128)(2,1)S(1)}, u32[]{:S(2)}, u32[]{:S(2)}) %all-to-all-start.2) | async-done | bytes 262176 | tf_op jit(solution)/shard_map/all_to_all | solution.py:81
  71.1 1.6 %fusion.14 = f32[16,96,256]{2,1,0:T(8,128)} fusion(bf16[16,96,32]{1,2,0:T(8,128)(2,1)S(1)} %all-to-all-done.1, bf16[16,32,256]{2,1,0:T(8,128)(2,1)S(1)} %all-to-all-done.2), kind=kOutput, calls=%fused_computation.23 | convolution fusion | flops 25952256 | bytes 1933312 | tf_op jit(solution)/shard_map/str,src->stc/dot_general | solution.py:82
  72.7 2.1 %reshape.53 = f32[1536,2,128]{2,1,0:T(2,128)S(1)} reshape(f32[16,96,256]{2,1,0:T(8,128)} %fusion.14) | data formatting | bytes 3145728 | tf_op jit(solution)/shard_map/convert_element_type | solution.py:86
  74.7 1.3 %fusion.13 = bf16[2,1536,128]{2,1,0:T(8,128)(2,1)S(1)} fusion(f32[1536,2,128]{2,1,0:T(2,128)S(1)} %reshape.53, bf16[2,1536,128]{2,1,0:T(8,128)(2,1)} %param.19), kind=kLoop, calls=%fused_computation.20 | loop fusion | flops 1179648 | bytes 3145728 | tf_op jit(solution)/shard_map/convert_element_type | solution.py:86
  76.0 4.9 %while.11 = (s32[]{:T(128)}, bf16[2,512,64]{1,2,0:T(8,128)(2,1)S(1)}, bf16[2,512,64]{2,1,0:T(8,128)(2,1)S(1)}, bf16[2,1536,128]{2,1,0:T(8,128)(2,1)S(1)}, s32[16]{0:T(128)S(1)}, /*index=5*/s32[]{:T(128)}) while((s32[]{:T(128)}, bf16[2,512,64]{1,2,0:T(8,128)(2,1)S(1)}, bf16[2,512,64]{2,1,0:T(8,128)(2,1)S(1)}, ...), condition=%wide.region_5.8_spmd.clone, body=%wide.region_2.7_spmd.clone.sunk | while | flops 207651328 | bytes 11223697 | solution.py:91
  76.2 0.7 fusion.71
  76.9 0.6 fusion.72
  77.5 1.0 %fusion.73 = bf16[2,512,64]{1,2,0:T(8,128)(2,1)S(1)} fusion(bf16[2,512,64]{1,2,0:T(8,128)(2,1)S(1)} %get-tuple-element.130, s32[]{:T(128)} %get-tuple-element.129, f32[512,1536]{1,0:T(8,128)S(1)} %get-tuple-element.121, f32[512]{0:T(512)S(1)} %fusion.72, f32[512]{0:T(512)S(1)} %get-tuple-element.122, ...), kind=kOutput, calls=%fused_computation.9.clone.1 | convolution fusion | flops 103055360 | bytes 3608580 | tf_op jit(solution)/shard_map/while/body/eval_jaxpr/while/body/eval_jaxpr/dot_general | solution.py:52
  78.7 0.7 fusion.71
  79.4 0.6 fusion.72
  80.0 1.0 %fusion.73 = bf16[2,512,64]{1,2,0:T(8,128)(2,1)S(1)} fusion(bf16[2,512,64]{1,2,0:T(8,128)(2,1)S(1)} %get-tuple-element.130, s32[]{:T(128)} %get-tuple-element.129, f32[512,1536]{1,0:T(8,128)S(1)} %get-tuple-element.121, f32[512]{0:T(512)S(1)} %fusion.72, f32[512]{0:T(512)S(1)} %get-tuple-element.122, ...), kind=kOutput, calls=%fused_computation.9.clone.1 | convolution fusion | flops 103055360 | bytes 3608580 | tf_op jit(solution)/shard_map/while/body/eval_jaxpr/while/body/eval_jaxpr/dot_general | solution.py:52
  81.0 0.2 copy.30
  81.1 0.1 reshape.50
  81.3 10.7 %all_to_all.20 = bf16[16,32,128]{2,1,0:T(8,128)(2,1)S(1)} all-to-all(bf16[16,32,128]{2,1,0:T(8,128)(2,1)S(1)} %reshape.50), channel_id=1, replica_groups=mesh['groups'=2,'tok'=16] {'tok'}, dimensions={0} | all-to-all | bytes 262144 | tf_op jit(solution)/shard_map/all_to_all | solution.py:93
  92.0 4.6 %convolution_convert_fusion.1 = bf16[32,1536]{1,0:T(8,128)(2,1)} fusion(bf16[2048,1536]{1,0:T(8,128)(2,1)} %param.20, bf16[4,8,16,128]{3,2,1,0:T(8,128)(2,1)S(1)} %bitcast.110), kind=kOutput, calls=%fused_computation.18 | convolution fusion | flops 201375744 | bytes 6520832 | tf_op jit(solution)/shard_map/dot_general | solution.py:96
  (27 shorter events, 1.0 us)
Async XLA Ops:
  0.0 2.6 %copy-start = (f32[4096,32]{0,1:T(8,128)S(1)}, f32[4096,32]{0,1:T(8,128)}, u32[]{:S(2)}) copy-start(f32[4096,32]{0,1:T(8,128)} %param.18) | copy-start | bytes 1572868
  21.7 16.6 %copy-start.1 = (bf16[32,2048]{1,0:T(8,128)(2,1)S(1)}, bf16[32,2048]{1,0:T(8,128)(2,1)}, u32[]{:S(2)}) copy-start(bf16[32,2048]{1,0:T(8,128)(2,1)} %param.13) | copy-start | bytes 393220
  30.9 15.3 %all-to-all-start.1 = ((bf16[16,96,32]{1,2,0:T(8,128)(2,1)}), bf16[16,96,32]{1,2,0:T(8,128)(2,1)S(1)}, u32[]{:S(2)}, u32[]{:S(2)}) async-start(bf16[16,96,32]{1,2,0:T(8,128)(2,1)} %stack.2), calls=%async_computation.1 | async-start | bytes 262144 | tf_op jit(solution)/shard_map/all_to_all | solution.py:14
  46.2 11.4 %all-to-all-start = ((bf16[16,32,128]{2,1,0:T(8,128)(2,1)}), bf16[16,32,128]{2,1,0:T(8,128)(2,1)S(1)}, u32[]{:S(2)}, u32[]{:S(2)}) async-start(bf16[16,32,128]{2,1,0:T(8,128)(2,1)} %bitcast.101), calls=%async_computation | async-start | bytes 262144 | tf_op jit(solution)/shard_map/all_to_all | solution.py:79
  57.6 13.5 %all-to-all-start.2 = ((bf16[16,32,256]{2,1,0:T(8,128)(2,1)}), bf16[16,32,256]{2,1,0:T(8,128)(2,1)S(1)}, u32[]{:S(2)}, u32[]{:S(2)}) async-start(bf16[16,32,256]{2,1,0:T(8,128)(2,1)} %bitcast.100), calls=%async_computation.2 | async-start | bytes 524288 | tf_op jit(solution)/shard_map/all_to_all | solution.py:81
  74.7 1.3 %copy-start.2 = (s32[16]{0:T(128)S(1)}, s32[16]{0:T(128)}, u32[]{:S(2)}) copy-start(s32[16]{0:T(128)} %param.17) | copy-start | bytes 196
